TPU v7x, 32 devices: a whole 2x2x4 slice. The times are simulated.
32 devices in a mesh: seq: 2 (over y), shard: 4 (over x, core), rep: 4 (over z).
Axes of the slice: x: 2, y: 2, z: 4, core: 2. Of those that a mesh axis runs over, the one named last changes fastest.
Arguments:
- tokens: bfloat16 [16, 580, 1024], P(('shard', 'rep'), 'seq'), may hold values from -6 to 6
- lengths: int32 [16], P(('shard', 'rep')), may hold values from 435 to 580, as said below
- qkv_weight: bfloat16 [1024, 3072], P('shard'), may hold values from -0.1875 to 0.1875
- query_bias: bfloat16 [1024], P('shard'), may hold values from -3 to 3
- value_bias: bfloat16 [1024], P('shard'), may hold values from -0.29882812 to 0.29882812
- out_weight: bfloat16 [1024, 1024], P('shard'), may hold values from -2 to 2
- out_bias: bfloat16 [1024], P('shard'), may hold values from -0.59765625 to 0.59765625
- first_gain: bfloat16 [1024], P('shard'), may hold values from 0.5 to 1.5
- first_shift: bfloat16 [1024], P('shard'), may hold values from -0.29882812 to 0.29882812
- second_gain: bfloat16 [1024], P('shard'), may hold values from 0.5 to 1.5
- second_shift: bfloat16 [1024], P('shard'), may hold values from -3 to 3
- up_weight: bfloat16 [1024, 4096], P('shard'), may hold values from -0.1875 to 0.1875
- up_bias: bfloat16 [4096], P('shard'), may hold values from -3 to 3
- down_weight: bfloat16 [4096, 1024], P('shard'), may hold values from -0.09375 to 0.09375
- down_bias: bfloat16 [1024], P('shard'), may hold values from -3 to 3
- cotangent: bfloat16 [16, 580, 1024], P(('shard', 'rep'), 'seq'), may hold values from -6 to 6
Outputs:
- block_out: bfloat16 [16, 580, 1024], P(('shard', 'rep'), 'seq')
- token_grad: float32 [16, 580, 1024], P(('shard', 'rep'), 'seq')
- grad_qkv_weight: float32 [1024, 3072], P('shard')
- grad_query_bias: float32 [1024], P('shard')
- grad_value_bias: float32 [1024], P('shard')
- grad_out_weight: float32 [1024, 1024], P('shard')
- grad_out_bias: float32 [1024], P('shard')
- grad_first_gain: float32 [1024], P('shard')
- grad_first_shift: float32 [1024], P('shard')
- grad_second_gain: float32 [1024], P('shard')
- grad_second_shift: float32 [1024], P('shard')
- grad_up_weight: float32 [1024, 4096], P('shard')
- grad_up_bias: float32 [4096], P('shard')
- grad_down_weight: float32 [4096, 1024], P('shard')
- grad_down_bias: float32 [1024], P('shard')
Inputs may be any that keep to these rules, and one draw needn't show every extreme that they name: Tokens of an image at positions lengths[image] and beyond are padding. Some image has 580 valid tokens and some has 435.
All inputs are finite; a program needn't handle non-finite values.
Results may differ from a plain program's by a relative error of at most 0.012.
Values may be sent and summed in bfloat16 or wider, within the bound.
No kernel may reach another device: no remote copies, remote signals or barrier semaphores. Data moves between devices by JAX's collectives and lax.ppermute only.
A program may use at most 192 MiB of HBM per device.

v0:
```python
import jax
import jax.numpy as jnp
from jax import lax
from jax.sharding import PartitionSpec as P

H = 16
HD = 64


def layer_norm(values, gain_vec, shift_vec):
    centered = values - jnp.mean(values, -1, keepdims=True)
    variance = jnp.mean(centered * centered, -1, keepdims=True)
    return centered * lax.rsqrt(variance + 1e-06) * gain_vec + shift_vec


def gelu_exact(values):
    return jax.nn.gelu(values, approximate=False)


def attention_scores(query_heads, key_heads, visible, score_scale):
    scores = (
        jnp.einsum("iqhd,ikhd->ihqk", query_heads, key_heads, preferred_element_type=jnp.float32)
        * score_scale
    )
    return jnp.where(visible[:, None, None, :], scores, -1000000000.0)


def single_out(values):
    return values.reshape((values.shape[0], 1) + values.shape[1:])


def merge_out(values):
    return values.reshape((values.shape[0] * values.shape[1],) + values.shape[2:])


def shards(
    tokens,
    lengths,
    qkv_weight,
    query_bias,
    value_bias,
    out_weight,
    out_bias,
    first_gain,
    first_shift,
    second_gain,
    second_shift,
    up_weight,
    up_bias,
    down_weight,
    down_bias,
    cotangent,
):
    images, rows_local, model_width = tokens.shape
    full_len = rows_local * lax.axis_size("seq")
    score_scale = HD ** (-0.5)
    gathered = (
        lax.all_gather(qkv_weight, "shard", axis=0, tiled=True),
        lax.all_gather(out_weight, "shard", axis=0, tiled=True),
        lax.all_gather(up_weight, "shard", axis=0, tiled=True),
        lax.all_gather(down_weight, "shard", axis=0, tiled=True),
        lax.all_gather(query_bias, "shard", axis=0, tiled=True),
        lax.all_gather(value_bias, "shard", axis=0, tiled=True),
        lax.all_gather(out_bias, "shard", axis=0, tiled=True),
        lax.all_gather(first_gain, "shard", axis=0, tiled=True),
        lax.all_gather(first_shift, "shard", axis=0, tiled=True),
        lax.all_gather(second_gain, "shard", axis=0, tiled=True),
        lax.all_gather(second_shift, "shard", axis=0, tiled=True),
        lax.all_gather(up_bias, "shard", axis=0, tiled=True),
        lax.all_gather(down_bias, "shard", axis=0, tiled=True),
    )
    wqkv, wout, wup, wdown = (gathered[0], gathered[1], gathered[2], gathered[3])
    vec_query, vec_value, vec_out, gain_one, shift_one, gain_two, shift_two, vec_up, vec_down = [
        item.astype(jnp.float32) for item in gathered[4:]
    ]
    flat_rows = tokens.reshape(-1, model_width).astype(jnp.float32)
    normed_first, pull_first = jax.vjp(layer_norm, flat_rows, gain_one, shift_one)
    first_low = normed_first.astype(jnp.bfloat16)
    projected = jnp.dot(first_low, wqkv, preferred_element_type=jnp.float32)
    queries = (projected[:, :model_width] + vec_query).astype(jnp.bfloat16)
    keys_local = projected[:, model_width : 2 * model_width].astype(jnp.bfloat16)
    values_local = (projected[:, 2 * model_width :] + vec_value).astype(jnp.bfloat16)
    keys_all, values_all = (
        lax.all_gather(
            keys_local.reshape(images, rows_local, model_width), "seq", axis=1, tiled=True
        ),
        lax.all_gather(
            values_local.reshape(images, rows_local, model_width), "seq", axis=1, tiled=True
        ),
    )
    query_heads = single_out(queries.reshape(images, rows_local, H, HD))
    key_heads = single_out(keys_all.reshape(images, full_len, H, HD))
    value_heads = single_out(values_all.reshape(images, full_len, H, HD))
    visible = single_out(jnp.arange(full_len, dtype=jnp.int32)[None, :] < lengths[:, None])

    def attend_forward(block):
        query_blk, key_blk, value_blk, visible_blk = block
        scores = attention_scores(query_blk, key_blk, visible_blk, score_scale)
        score_top = jnp.max(scores, -1, keepdims=True)
        shifted = jnp.exp(scores - score_top)
        exp_total = jnp.sum(shifted, -1, keepdims=True)
        log_total = score_top + jnp.log(exp_total)
        weights_low = (shifted / exp_total).astype(jnp.bfloat16)
        mixed_blk = jnp.einsum(
            "ihqk,ikhd->iqhd", weights_low, value_blk, preferred_element_type=jnp.float32
        )
        return (mixed_blk.astype(jnp.bfloat16), log_total)

    mixed_out, log_totals = lax.map(attend_forward, (query_heads, key_heads, value_heads, visible))
    mixed_low = mixed_out.reshape(-1, model_width)
    middle = flat_rows + jnp.dot(mixed_low, wout, preferred_element_type=jnp.float32) + vec_out
    normed_second, pull_second = jax.vjp(layer_norm, middle, gain_two, shift_two)
    second_low = normed_second.astype(jnp.bfloat16)
    hidden = jnp.dot(second_low, wup, preferred_element_type=jnp.float32) + vec_up
    activated, pull_gelu = jax.vjp(gelu_exact, hidden)
    act_low = activated.astype(jnp.bfloat16)
    result = middle + jnp.dot(act_low, wdown, preferred_element_type=jnp.float32) + vec_down
    block_out = result.astype(jnp.bfloat16).reshape(tokens.shape)
    back_qkv, back_out, back_up, back_down = (
        lax.all_gather(qkv_weight, "shard", axis=0, tiled=True),
        lax.all_gather(out_weight, "shard", axis=0, tiled=True),
        lax.all_gather(up_weight, "shard", axis=0, tiled=True),
        lax.all_gather(down_weight, "shard", axis=0, tiled=True),
    )
    incoming = cotangent.reshape(-1, model_width)
    incoming_f = incoming.astype(jnp.float32)
    grad_down = jnp.dot(act_low.T, incoming, preferred_element_type=jnp.float32)
    grad_down_bias = jnp.sum(incoming_f, 0)
    grad_act = jnp.dot(incoming, back_down.T, preferred_element_type=jnp.float32)
    hidden_low = pull_gelu(grad_act)[0].astype(jnp.bfloat16)
    grad_up = jnp.dot(second_low.T, hidden_low, preferred_element_type=jnp.float32)
    grad_up_bias = jnp.sum(hidden_low.astype(jnp.float32), 0)
    grad_second = jnp.dot(hidden_low, back_up.T, preferred_element_type=jnp.float32)
    middle_norm, grad_gain_two, grad_shift_two = pull_second(grad_second)
    grad_middle = incoming_f + middle_norm
    branch_low = grad_middle.astype(jnp.bfloat16)
    grad_out = jnp.dot(mixed_low.T, branch_low, preferred_element_type=jnp.float32)
    grad_out_bias = jnp.sum(branch_low.astype(jnp.float32), 0)
    grad_mixed = (
        jnp.dot(branch_low, back_out.T, preferred_element_type=jnp.float32)
        .astype(jnp.bfloat16)
        .reshape(images, rows_local, H, HD)
    )

    def attend_backward(block):
        query_blk, key_blk, value_blk, visible_blk, mixed_grad_blk, log_blk = block
        scores = attention_scores(query_blk, key_blk, visible_blk, score_scale)
        weights_exact = jnp.exp(scores - log_blk)
        grad_weights = jnp.einsum(
            "iqhd,ikhd->ihqk", mixed_grad_blk, value_blk, preferred_element_type=jnp.float32
        )
        row_inner = jnp.sum(weights_exact * grad_weights, -1, keepdims=True)
        grad_scores = (weights_exact * (grad_weights - row_inner)).astype(jnp.bfloat16)
        query_grad_blk = (
            jnp.einsum("ihqk,ikhd->iqhd", grad_scores, key_blk, preferred_element_type=jnp.float32)
            * score_scale
        )
        key_blk_part = (
            jnp.einsum(
                "ihqk,iqhd->ikhd", grad_scores, query_blk, preferred_element_type=jnp.float32
            )
            * score_scale
        )
        value_blk_part = jnp.einsum(
            "ihqk,iqhd->ikhd",
            weights_exact.astype(jnp.bfloat16),
            mixed_grad_blk,
            preferred_element_type=jnp.float32,
        )
        return (query_grad_blk, key_blk_part, value_blk_part)

    grad_queries, key_part, value_part = lax.map(
        attend_backward,
        (query_heads, key_heads, value_heads, visible, single_out(grad_mixed), log_totals),
    )
    key_part = merge_out(key_part)
    value_part = merge_out(value_part)
    grad_keys, grad_values = (
        lax.psum_scatter(key_part, "seq", scatter_dimension=1, tiled=True),
        lax.psum_scatter(value_part, "seq", scatter_dimension=1, tiled=True),
    )
    query_low = grad_queries.reshape(-1, model_width).astype(jnp.bfloat16)
    value_low = grad_values.reshape(-1, model_width).astype(jnp.bfloat16)
    grad_proj = jnp.concatenate(
        [query_low, grad_keys.reshape(-1, model_width).astype(jnp.bfloat16), value_low], axis=1
    )
    grad_qkv = jnp.dot(first_low.T, grad_proj, preferred_element_type=jnp.float32)
    grad_query_bias = jnp.sum(query_low.astype(jnp.float32), 0)
    grad_value_bias = jnp.sum(value_low.astype(jnp.float32), 0)
    grad_first = jnp.dot(grad_proj, back_qkv.T, preferred_element_type=jnp.float32)
    flat_norm, grad_gain_one, grad_shift_one = pull_first(grad_first)
    token_grad = (grad_middle + flat_norm).reshape(tokens.shape)
    owned_grads = (
        lax.psum_scatter(grad_qkv, "shard", scatter_dimension=0, tiled=True),
        lax.psum_scatter(grad_query_bias, "shard", scatter_dimension=0, tiled=True),
        lax.psum_scatter(grad_value_bias, "shard", scatter_dimension=0, tiled=True),
        lax.psum_scatter(grad_out, "shard", scatter_dimension=0, tiled=True),
        lax.psum_scatter(grad_out_bias, "shard", scatter_dimension=0, tiled=True),
        lax.psum_scatter(grad_gain_one, "shard", scatter_dimension=0, tiled=True),
        lax.psum_scatter(grad_shift_one, "shard", scatter_dimension=0, tiled=True),
        lax.psum_scatter(grad_gain_two, "shard", scatter_dimension=0, tiled=True),
        lax.psum_scatter(grad_shift_two, "shard", scatter_dimension=0, tiled=True),
        lax.psum_scatter(grad_up, "shard", scatter_dimension=0, tiled=True),
        lax.psum_scatter(grad_up_bias, "shard", scatter_dimension=0, tiled=True),
        lax.psum_scatter(grad_down, "shard", scatter_dimension=0, tiled=True),
        lax.psum_scatter(grad_down_bias, "shard", scatter_dimension=0, tiled=True),
    )
    summed = lax.psum(
        (
            owned_grads[0],
            owned_grads[1],
            owned_grads[2],
            owned_grads[3],
            owned_grads[4],
            owned_grads[5],
            owned_grads[6],
            owned_grads[7],
            owned_grads[8],
            owned_grads[9],
            owned_grads[10],
            owned_grads[11],
            owned_grads[12],
        ),
        ("seq", "rep"),
    )
    return (
        block_out,
        token_grad,
        summed[0],
        summed[1],
        summed[2],
        summed[3],
        summed[4],
        summed[5],
        summed[6],
        summed[7],
        summed[8],
        summed[9],
        summed[10],
        summed[11],
        summed[12],
    )


def solution(mesh):
    return jax.shard_map(
        shards,
        mesh=mesh,
        in_specs=(
            P(("shard", "rep"), "seq", None),
            P(("shard", "rep")),
            P("shard", None),
            P("shard"),
            P("shard"),
            P("shard", None),
            P("shard"),
            P("shard"),
            P("shard"),
            P("shard"),
            P("shard"),
            P("shard", None),
            P("shard"),
            P("shard", None),
            P("shard"),
            P(("shard", "rep"), "seq", None),
        ),
        out_specs=(
            P(("shard", "rep"), "seq", None),
            P(("shard", "rep"), "seq", None),
            P("shard", None),
            P("shard"),
            P("shard"),
            P("shard", None),
            P("shard"),
            P("shard"),
            P("shard"),
            P("shard"),
            P("shard"),
            P("shard", None),
            P("shard"),
            P("shard", None),
            P("shard"),
        ),
        check_vma=False,
    )
```

profile of v0, /device:TPU:0, one launch (start us, length us, event | category | flops | bytes accessed | tf_op | source)
XLA Modules:
  0.0 1235.9 jit_solution(14504747822557526560)
XLA Ops:
  9.3 6.0 all-gather.3
  15.3 5.4 all-gather.2
  20.7 1.3 convert_reduce_fusion.4
  22.0 1.4 fusion.32
  23.4 35.2 %all-gather.19.cloned.1.call-done = bf16[1024,3072]{1,0:T(8,128)(2,1)} async-done(((bf16[256,3072]{1,0:T(8,128)(2,1)}), bf16[1024,3072]{1,0:T(8,128)(2,1)}) %all-gather.19.cloned.1.call-update) | async-done | bytes 6291472 | tf_op jit(solution)/shard_map/all_gather | solution.py:58
  58.7 5.2 fusion.56
  63.9 1.8 copy-done.17
  65.7 0.9 fusion.40
  66.8 5.1 all-gather.4
  71.8 5.1 all-gather.6
  76.9 2.8 fusion.34
  82.3 5.1 all-gather.10
  87.3 5.1 all-gather.9
  92.4 5.1 all-gather.8
  97.5 5.7 all_gather.61
  103.6 4.9 copy.47
  108.4 3.6 reshape.246
  112.0 3.2 all-gather.27.cloned.1.call-done
  115.2 4.9 copy.45
  120.1 4.5 reshape.243
  124.6 2.3 fusion.6
  126.9 3.3 fusion
  130.2 1.2 copy-done
  131.4 3.9 fusion.23
  135.4 3.9 all-gather.21.cloned.1.call-done
  139.2 2.5 fusion.64
  142.1 56.9 %all-gather.23.cloned.1.call-done = bf16[1024,4096]{1,0:T(8,128)(2,1)} async-done(((bf16[256,4096]{1,0:T(8,128)(2,1)}), bf16[1024,4096]{1,0:T(8,128)(2,1)}) %all-gather.23.cloned.1.call-update) | async-done | bytes 8388624 | tf_op jit(solution)/shard_map/all_gather | solution.py:60
  198.9 17.7 %multiply_convert_fusion.1 = (bf16[290,4096]{1,0:T(8,128)(2,1)}, f32[290,4096]{1,0:T(8,128)}, f32[290,4096]{1,0:T(8,128)}) fusion(f32[4096]{0:T(1024)S(1)} %convert_element_type.150, bf16[1024,4096]{1,0:T(8,128)(2,1)} %all-gather.23.cloned.1.call-done, f32[290,1024]{1,0:T(8,128)S(1)} %get-tuple-element.157, f32[1024]{0:T(1024)S(1)} %bitcast.156, ...), kind=kOutput, calls=%fused_computation.17 | convolution fusion | flops 2512578560 | bytes 21481744 | tf_op jit(solution)/shard_map/dot_general | solution.py:114
  216.6 42.1 %all-gather.25.cloned.1.call-done = bf16[4096,1024]{1,0:T(8,128)(2,1)} async-done(((bf16[1024,1024]{1,0:T(8,128)(2,1)}), bf16[4096,1024]{1,0:T(8,128)(2,1)}) %all-gather.25.cloned.1.call-update) | async-done | bytes 8388624 | tf_op jit(solution)/shard_map/all_gather | solution.py:61
  258.7 10.7 convert_reduce_fusion
  269.3 6.4 multiply_reduce_fusion.1
  276.2 1.1 copy-done.5
  278.4 3.3 fusion.65
  283.6 3.2 convolution_convert_fusion
  286.8 1.5 copy.48
  288.3 8.7 fusion.13
  297.1 10.0 multiply_reduce_fusion
  307.1 6.5 multiply_convert_fusion
  313.6 2.6 copy-done.1
  316.2 2.8 multiply_bitcast_fusion
  319.0 125.6 %all-reduce.19 = (bf16[1,580,16,64]{1,3,2,0:T(8,128)(2,1)}, bf16[1,580,16,64]{1,3,2,0:T(8,128)(2,1)}) all-reduce(f32[1,580,16,64]{1,3,2,0:T(8,128)} %fusion.13, f32[1,580,16,64]{1,3,2,0:T(8,128)} %multiply_bitcast_fusion), channel_id=5, replica_groups=mesh['seq'=2,'shard'=4,'rep'=4] {'seq'}, use_global_device_ids=true, to_apply=%region_10.11.clone | all-reduce | flops 1187840 | bytes 7127040
  444.6 1.9 convert_reduce_fusion.1
  446.5 1.9 dynamic-slice_convert_fusion.1
  448.3 5.0 convert_reduce_fusion.2
  454.2 9.4 fusion.36
  463.7 13.5 %fusion.59 = f32[1024,4096]{1,0:T(8,128)} fusion(bf16[290,4096]{1,0:T(8,128)(2,1)} %copy-done.18, f32[290,1024]{1,0:T(8,128)S(1)} %get-tuple-element.157, f32[1024]{0:T(1024)S(1)} %bitcast.157, f32[1024]{0:T(1024)S(1)} %bitcast.155, f32[290]{0:T(512)S(1)} %fusion.48, f32[290]{0:T(512)S(1)} %broadcast_multiply_fusion), kind=kOutput, calls=%fused_computation.105 | convolution fusion | flops 2434181120 | bytes 20351248 | tf_op jit(solution)/shard_map/dot_general | solution.py:131
  477.3 1.1 copy-done.8
  478.4 10.4 fusion.41
  488.9 73.8 %reduce-scatter.7.cloned.1.call-done = f32[256,3072]{1,0:T(8,128)} async-done(((f32[1024,3072]{1,0:T(8,128)}), f32[256,3072]{1,0:T(8,128)}) %reduce-scatter.7.cloned.1.call-update) | async-done | bytes 3145744 | tf_op jit(solution)/shard_map/reduce_scatter | solution.py:194
  562.7 127.7 %reduce-scatter.11.cloned.1.call-done = f32[256,4096]{1,0:T(8,128)} async-done(((f32[1024,4096]{1,0:T(8,128)}), f32[256,4096]{1,0:T(8,128)}) %reduce-scatter.11.cloned.1.call-update) | async-done | bytes 4194320 | tf_op jit(solution)/shard_map/reduce_scatter | solution.py:203
  690.4 127.5 %reduce-scatter.13.cloned.1.call-done = f32[1024,1024]{1,0:T(8,128)} async-done(((f32[4096,1024]{1,0:T(8,128)}), f32[1024,1024]{1,0:T(8,128)}) %reduce-scatter.13.cloned.1.call-update) | async-done | bytes 4194320 | tf_op jit(solution)/shard_map/reduce_scatter | solution.py:205
  820.4 5.2 all-gather.11
  825.8 7.2 fusion.60
  833.7 1.6 convert_reduce_fusion.3
  835.4 11.6 all-reduce.13
  847.6 3.5 copy.49
  851.2 39.8 %all-reduce.11 = (f32[256]{0:T(256)}, f32[256]{0:T(256)}, f32[256]{0:T(256)}, f32[256]{0:T(256)}, f32[256]{0:T(256)}, /*index=5*/f32[256]{0:T(256)}, f32[256]{0:T(256)}, f32[1024]{0:T(1024)}, f32[256]{0:T(256)}) all-reduce(f32[256]{0:T(256)S(1)} %dynamic-slice.7, ...), channel_id=1, replica_groups=mesh['seq'=2,'shard'=4,'rep'=4] {'seq','rep'}, use_global_device_ids=true, to_apply=%region_17.18 | all-reduce | flops 3072 | bytes 24576 | tf_op jit(solution)/shard_map/psum | solution.py:208
  890.9 7.6 fusion.28
  898.6 319.8 %all-reduce.18.cloned.1.call-done = (f32[256,3072]{1,0:T(8,128)}, f32[256,1024]{1,0:T(8,128)}, f32[256,4096]{1,0:T(8,128)}, f32[1024,1024]{1,0:T(8,128)}) async-done(((f32[256,3072]{1,0:T(8,128)}, f32[256,1024]{1,0:T(8,128)}, f32[256,4096]{1,0:T(8,128)}, f32[1024,1024]{1,0:T(8,128)}), (f32[256,3072]{1,0:T(8,128)}, f32[256,1024]{1,0:T(8,128)}, f32[256,4096]{1,0:T(8,128)}, ...) | async-done | bytes 12582928 | tf_op jit(solution)/shard_map/psum | solution.py:208
  1218.4 4.0 copy.63
  1222.4 1.0 copy.64
  1223.4 2.1 copy.65
  1225.6 1.6 copy-done.11
  1227.1 2.0 copy.66
  (136 shorter events, 11.3 us)
Async XLA Ops:
  7.2 51.5 %all-gather.19.cloned.1.call-start = ((), (), s32[]{:S(2)}) async-start(), calls=%async_computation.4 | async-start | bytes 7864320 | tf_op jit(solution)/shard_map/all_gather | solution.py:58
  7.9 95.6 %all-gather.29.cloned.1.call-start = ((), (), s32[]{:S(2)}) async-start(), calls=%async_computation.13 | async-start | bytes 1818624 | tf_op jit(solution)/shard_map/all_gather | solution.py:84
  23.4 40.5 %copy-start.22 = (f32[290]{0:T(512)}, f32[290]{0:T(512)S(1)}, u32[]{:S(2)}) copy-start(f32[290]{0:T(512)S(1)} %fusion.32) | copy-start | bytes 3484
  58.7 8.1 copy-start.25
  58.7 8.1 copy-start.26
  63.9 1.8 copy-start.17
  66.7 48.6 %all-gather.27.cloned.1.call-start = ((), (), s32[]{:S(2)}) async-start(), calls=%async_computation.12 | async-start | bytes 1818624 | tf_op jit(solution)/shard_map/all_gather | solution.py:87
  76.9 5.3 copy-start.27
  76.9 5.3 copy-start.28
  76.9 5.3 copy-start.29
  76.9 20.5 %copy-start.24 = (bf16[1024]{0:T(1024)(128)(2,1)S(1)}, bf16[1024]{0:T(1024)(128)(2,1)}, u32[]{:S(2)}) copy-start(bf16[1024]{0:T(1024)(128)(2,1)} %param.28) | copy-start | bytes 6148
  79.8 59.5 %all-gather.21.cloned.1.call-start = ((), (), s32[]{:S(2)}) async-start(), calls=%async_computation.5 | async-start | bytes 2621440 | tf_op jit(solution)/shard_map/all_gather | solution.py:59
  80.3 118.6 %all-gather.23.cloned.1.call-start = ((), (), s32[]{:S(2)}) async-start(), calls=%async_computation.6 | async-start | bytes 10485760 | tf_op jit(solution)/shard_map/all_gather | solution.py:60
  80.9 177.7 %all-gather.25.cloned.1.call-start = ((), (), s32[]{:S(2)}) async-start(), calls=%async_computation.7 | async-start | bytes 10485760 | tf_op jit(solution)/shard_map/all_gather | solution.py:61
  81.5 407.4 %reduce-scatter.9.cloned.1.call-start = ((), (), s32[]{:S(2)}) async-start(), calls=%async_computation.9 | async-start | bytes 5242880 | tf_op jit(solution)/shard_map/reduce_scatter | solution.py:197
  112.0 14.9 %copy-start.3 = (bf16[580,16,64]{0,2,1:T(8,128)(2,1)}, bf16[580,16,64]{0,2,1:T(8,128)(2,1)S(1)}, u32[]{:S(2)}) copy-start(bf16[580,16,64]{0,2,1:T(8,128)(2,1)S(1)} %reshape.246) | copy-start | bytes 3563524
  126.9 4.5 copy-start
  126.9 4.5 copy-start.9
  131.4 7.8 copy-start.2
  269.3 6.4 copy-start.18
  269.3 7.9 copy-start.7
  276.2 1.1 copy-start.5
  277.6 0.8 copy-start.19
  281.6 0.7 copy-start.32
  281.6 1.9 copy-start.20
  281.7 281.0 %reduce-scatter.7.cloned.1.call-start = ((), (), s32[]{:S(2)}) async-start(), calls=%async_computation.8 | async-start | bytes 15728640 | tf_op jit(solution)/shard_map/reduce_scatter | solution.py:194
  288.3 8.7 copy-start.10
  288.3 18.7 %slice-start = ((s8[12124160]{0:T(1024)(128)(4,1)}), s8[4194304]{0:T(1024)(128)(4,1)S(1)}, s32[]{:S(2)}) async-start(s8[12124160]{0:T(1024)(128)(4,1)} %bitcast.131), calls=%async_computation.15 | async-start | bytes 8388608
  288.3 18.7 %slice-start.1 = ((s8[12124160]{0:T(1024)(128)(4,1)}), s8[4194304]{0:T(1024)(128)(4,1)S(1)}, s32[]{:S(2)}) async-start(s8[12124160]{0:T(1024)(128)(4,1)} %bitcast.131), calls=%async_computation.16 | async-start | bytes 8388608
  297.1 10.0 slice-start.2
  313.6 2.6 copy-start.1
  319.0 129.3 %copy-start.4 = (bf16[580,16,64]{0,2,1:T(8,128)(2,1)S(1)}, bf16[580,16,64]{0,2,1:T(8,128)(2,1)}, u32[]{:S(2)}) copy-start(bf16[580,16,64]{0,2,1:T(8,128)(2,1)} %copy-done.3) | copy-start | bytes 3563524
  446.4 6.9 copy-start.15
  448.3 5.0 copy-start.16
  453.4 0.9 copy-start.13
  463.7 226.7 %reduce-scatter.11.cloned.1.call-start = ((), (), s32[]{:S(2)}) async-start(), calls=%async_computation.10 | async-start | bytes 20971520 | tf_op jit(solution)/shard_map/reduce_scatter | solution.py:203
  477.2 1.2 copy-start.8
  477.2 340.6 %reduce-scatter.13.cloned.1.call-start = ((), (), s32[]{:S(2)}) async-start(), calls=%async_computation.11 | async-start | bytes 20971520 | tf_op jit(solution)/shard_map/reduce_scatter | solution.py:205
  488.8 729.6 %all-reduce.18.cloned.1.call-start = ((), (), s32[]{:S(2)}) async-start(), calls=%async_computation.14 | async-start | bytes 25165824 | tf_op jit(solution)/shard_map/psum | solution.py:208
  817.9 0.7 copy-start.31
  817.9 2.5 copy-start.30
  817.9 7.9 copy-start.14
  825.8 7.2 copy-start.23
  825.8 7.9 copy-start.6
  1218.4 4.0 copy-start.21
  1218.4 5.0 copy-start.12
  1223.4 3.7 copy-start.11
Sparse Core Ops, SparseCore 0:
  9.5 49.0 all-gather.18
  66.8 23.1 all-gather.28
  92.1 23.1 all-gather.26
  116.6 22.5 all-gather.20
  140.6 58.2 all-gather.22
  200.4 58.2 all-gather.24
  281.8 44.5 reduce-scatter.8
  463.8 98.8 reduce-scatter.6
  565.3 125.0 reduce-scatter.10
  692.8 125.0 reduce-scatter.12
  822.6 395.7 all-reduce.17
where the time goes:
time: 1240 us
  waiting for transfers between devices  792 us (64%)
  blocking collectives  225 us (18%)
  matrix products  130 us (10%)
  local copies, waits for them, and re-layouts  50.5 us (4%)
  other arithmetic  20.7 us (2%)
  between operations  17.2 us (1%)
    psum x1, waiting for transfers between devices, shards(): lax.psum((owned_grads[0], owned_grads[1], owned_grads[2], owned_grads[3],...  320 us
    unnamed x2, blocking collectives  137 us
    reduce_scatter x1, waiting for transfers between devices, shards(): lax.psum_scatter(grad_up, 'shard', scatter_dimension=0, tiled=True)  128 us
    reduce_scatter x1, waiting for transfers between devices, shards(): lax.psum_scatter(grad_down, 'shard', scatter_dimension=0, tiled=True)  128 us
    reduce_scatter x1, waiting for transfers between devices, shards(): lax.psum_scatter(grad_qkv, 'shard', scatter_dimension=0, tiled=True)  73.8 us
    all_gather x1, waiting for transfers between devices, shards(): lax.all_gather(up_weight, 'shard', axis=0, tiled=True)  56.9 us
    all_gather x1, waiting for transfers between devices, shards(): lax.all_gather(down_weight, 'shard', axis=0, tiled=True)  42.1 us
    psum x1, blocking collectives, shards(): lax.psum((owned_grads[0], owned_grads[1], owned_grads[2], owned_grads[3],...  39.8 us
  transfers between devices with their start and end apart: 11, of which 9 were waited for; matrix products, arithmetic and copies ran while one was open for 12% of the time, Pallas kernels for 0%

commit v1 on v0

--- a/solution.py
+++ b/solution.py
@@ -5,6 +5,24 @@
 
 H = 16
 HD = 64
+
+
+def gather_around(shard, axis, dim):
+    ways, here, hop = (lax.axis_size(axis), lax.axis_index(axis), shard.shape[dim])
+    shape = [n * ways if d == dim else n for d, n in enumerate(shard.shape)]
+    full = lax.dynamic_update_slice_in_dim(
+        jnp.zeros(shape, shard.dtype), shard, here * hop, axis=dim
+    )
+    going_up = going_down = shard
+    for far in range(1, ways // 2 + 1):
+        going_up = lax.ppermute(going_up, axis, [(d, (d + 1) % ways) for d in range(ways)])
+        full = lax.dynamic_update_slice_in_dim(full, going_up, (here - far) % ways * hop, axis=dim)
+        if 2 * far < ways:
+            going_down = lax.ppermute(going_down, axis, [(d, (d - 1) % ways) for d in range(ways)])
+            full = lax.dynamic_update_slice_in_dim(
+                full, going_down, (here + far) % ways * hop, axis=dim
+            )
+    return full
 
 
 def layer_norm(values, gain_vec, shift_vec):
@@ -55,7 +73,7 @@
     full_len = rows_local * lax.axis_size("seq")
     score_scale = HD ** (-0.5)
     gathered = (
-        lax.all_gather(qkv_weight, "shard", axis=0, tiled=True),
+        gather_around(qkv_weight, "shard", 0),
         lax.all_gather(out_weight, "shard", axis=0, tiled=True),
         lax.all_gather(up_weight, "shard", axis=0, tiled=True),
         lax.all_gather(down_weight, "shard", axis=0, tiled=True),

time: 1240 us -> 1310 us (1.056)
  waiting for transfers between devices: 792 us -> 835 us
  blocking collectives: 225 us -> 239 us
    ppermute x0 -> x3, waiting for transfers between devices: none -> 31.4 us  [the longest x2 31.4 us: gather_around(): lax.ppermute(going_up, axis, [(d, (d + 1) % ways) for d in range(ways)])]
    unnamed x97 -> x95, local copies, waits for them, and re-layouts: 28.9 us -> 30.4 us
  transfers between devices with their start and end apart: 11 -> 14, of which waited for: 9 -> 10; matrix products, arithmetic and copies ran while one was open for 12% -> 12% of each run, Pallas kernels for 0% -> 0%
where the time goes in v1:
time: 1310 us; the launch traced here: 1300 us
  waiting for transfers between devices  835 us (64%)
  blocking collectives  239 us (18%)
  matrix products  126 us (10%)
  local copies, waits for them, and re-layouts  58.7 us (4%)
  other arithmetic  20.6 us (2%)
  between operations  17.2 us (1%)
    psum x1, waiting for transfers between devices, shards(): lax.psum((owned_grads[0], owned_grads[1], owned_grads[2], owned_grads[3],...  329 us
    unnamed x2, blocking collectives  137 us
    reduce_scatter x1, waiting for transfers between devices, shards(): lax.psum_scatter(grad_down, 'shard', scatter_dimension=0, tiled=True)  128 us
    reduce_scatter x1, waiting for transfers between devices, shards(): lax.psum_scatter(grad_up, 'shard', scatter_dimension=0, tiled=True)  128 us
    reduce_scatter x1, waiting for transfers between devices, shards(): lax.psum_scatter(grad_qkv, 'shard', scatter_dimension=0, tiled=True)  73 us
    all_gather x1, waiting for transfers between devices, shards(): lax.all_gather(up_weight, 'shard', axis=0, tiled=True)  56.9 us
    all_gather x1, waiting for transfers between devices, shards(): lax.all_gather(down_weight, 'shard', axis=0, tiled=True)  42 us
    psum x1, blocking collectives, shards(): lax.psum((owned_grads[0], owned_grads[1], owned_grads[2], owned_grads[3],...  39.9 us
  transfers between devices with their start and end apart: 14, of which 10 were waited for; matrix products, arithmetic and copies ran while one was open for 12% of the time, Pallas kernels for 0%

profile of v1, /device:TPU:0, one launch (start us, length us, event | category | flops | bytes accessed | tf_op | source)
XLA Modules:
  0.0 1302.2 jit_solution(14568019921382302746)
XLA Ops:
  7.8 2.0 collective-permute-start.1
  11.0 31.4 %collective-permute-done = bf16[256,3072]{1,0:T(8,128)(2,1)} collective-permute-done((bf16[256,3072]{1,0:T(8,128)(2,1)}, bf16[256,3072]{1,0:T(8,128)(2,1)}, u32[]{:S(2)}, u32[]{:S(2)}) %collective-permute-start) | collective-permute-done | bytes 1572896 | tf_op jit(solution)/shard_map/ppermute | solution.py:18
  42.4 2.4 collective-permute-start.2
  45.5 17.8 %all-gather.2 = bf16[4,1,256]{2,1,0:T(2,128)(2,1)S(1)} all-gather(bf16[1,1,256]{2,1,0:T(2,128)(2,1)S(1)} %reshape.256), channel_id=1, replica_groups=mesh['seq'=2,'shard'=4,'rep'=4] {'shard'}, dimensions={0}, use_global_device_ids=true | all-gather | bytes 2560 | tf_op jit(solution)/shard_map/all_gather | solution.py:83
  64.0 8.0 all-gather.3
  74.4 1.7 constant_dynamic-update-slice_fusion.2
  76.1 1.6 constant_dynamic-update-slice_fusion.1
  77.7 1.6 constant_dynamic-update-slice_fusion
  79.3 2.3 fusion.56
  81.6 1.8 copy-done.16
  84.4 5.2 all-gather.4
  89.7 5.1 all-gather.6
  94.8 2.8 fusion.34
  100.3 5.1 all-gather.8
  105.3 5.1 all-gather.9
  110.4 5.1 all-gather.10
  115.5 5.7 all_gather.59
  121.6 4.9 copy.47
  126.5 4.5 reshape.246
  130.9 2.9 all-gather.27.cloned.1.call-done
  133.8 4.9 copy.45
  138.7 4.5 reshape.243
  143.1 3.7 fusion.6
  146.8 3.3 fusion
  151.4 3.9 fusion.23
  155.3 2.7 all-gather.19.cloned.1.call-done
  157.9 2.5 fusion.64
  160.8 56.9 %all-gather.21.cloned.1.call-done = bf16[1024,4096]{1,0:T(8,128)(2,1)} async-done(((bf16[256,4096]{1,0:T(8,128)(2,1)}), bf16[1024,4096]{1,0:T(8,128)(2,1)}) %all-gather.21.cloned.1.call-update) | async-done | bytes 8388624 | tf_op jit(solution)/shard_map/all_gather | solution.py:78
  217.7 17.7 %multiply_convert_fusion.1 = (bf16[290,4096]{1,0:T(8,128)(2,1)}, f32[290,4096]{1,0:T(8,128)}, f32[290,4096]{1,0:T(8,128)}) fusion(f32[4096]{0:T(1024)S(1)} %convert_element_type.150, bf16[1024,4096]{1,0:T(8,128)(2,1)} %all-gather.21.cloned.1.call-done, f32[290,1024]{1,0:T(8,128)S(1)} %get-tuple-element.157, f32[1024]{0:T(1024)S(1)} %bitcast.156, ...), kind=kOutput, calls=%fused_computation.17 | convolution fusion | flops 2512578560 | bytes 21481744 | tf_op jit(solution)/shard_map/dot_general | solution.py:132
  235.3 42.0 %all-gather.23.cloned.1.call-done = bf16[4096,1024]{1,0:T(8,128)(2,1)} async-done(((bf16[1024,1024]{1,0:T(8,128)(2,1)}), bf16[4096,1024]{1,0:T(8,128)(2,1)}) %all-gather.23.cloned.1.call-update) | async-done | bytes 8388624 | tf_op jit(solution)/shard_map/all_gather | solution.py:79
  277.4 10.7 convert_reduce_fusion
  288.0 6.4 multiply_reduce_fusion.1
  297.1 3.3 fusion.65
  302.3 3.2 convolution_convert_fusion
  305.5 1.5 copy.48
  307.1 12.6 multiply_reduce_fusion
  319.6 1.5 slice-done.2
  321.1 6.5 multiply_convert_fusion
  327.7 2.6 copy-done.1
  330.3 2.8 multiply_bitcast_fusion
  333.1 4.4 fusion.13
  337.4 125.4 %all-reduce.19 = (bf16[1,580,16,64]{1,3,2,0:T(8,128)(2,1)}, bf16[1,580,16,64]{1,3,2,0:T(8,128)(2,1)}) all-reduce(f32[1,580,16,64]{1,3,2,0:T(8,128)} %fusion.13, f32[1,580,16,64]{1,3,2,0:T(8,128)} %multiply_bitcast_fusion), channel_id=5, replica_groups=mesh['seq'=2,'shard'=4,'rep'=4] {'seq'}, use_global_device_ids=true, to_apply=%region_10.11.clone | all-reduce | flops 1187840 | bytes 7127040
  462.8 1.9 convert_reduce_fusion.1
  464.7 1.9 dynamic-slice_convert_fusion.1
  466.6 5.0 convert_reduce_fusion.2
  472.5 9.4 fusion.36
  482.0 13.8 %fusion.59 = f32[1024,4096]{1,0:T(8,128)} fusion(bf16[290,4096]{1,0:T(8,128)(2,1)} %copy-done.17, f32[290,1024]{1,0:T(8,128)S(1)} %get-tuple-element.157, f32[1024]{0:T(1024)S(1)} %bitcast.157, f32[1024]{0:T(1024)S(1)} %bitcast.155, f32[290]{0:T(512)S(1)} %fusion.48, f32[290]{0:T(512)S(1)} %broadcast_multiply_fusion), kind=kOutput, calls=%fused_computation.109 | convolution fusion | flops 2434181120 | bytes 20351248 | tf_op jit(solution)/shard_map/dot_general | solution.py:149
  496.9 10.4 fusion.41
  508.0 73.0 %reduce-scatter.7.cloned.1.call-done = f32[256,3072]{1,0:T(8,128)} async-done(((f32[1024,3072]{1,0:T(8,128)}), f32[256,3072]{1,0:T(8,128)}) %reduce-scatter.7.cloned.1.call-update) | async-done | bytes 3145744 | tf_op jit(solution)/shard_map/reduce_scatter | solution.py:212
  581.0 127.7 %reduce-scatter.11.cloned.1.call-done = f32[256,4096]{1,0:T(8,128)} async-done(((f32[1024,4096]{1,0:T(8,128)}), f32[256,4096]{1,0:T(8,128)}) %reduce-scatter.11.cloned.1.call-update) | async-done | bytes 4194320 | tf_op jit(solution)/shard_map/reduce_scatter | solution.py:221
  708.7 127.7 %reduce-scatter.13.cloned.1.call-done = f32[1024,1024]{1,0:T(8,128)} async-done(((f32[4096,1024]{1,0:T(8,128)}), f32[1024,1024]{1,0:T(8,128)}) %reduce-scatter.13.cloned.1.call-update) | async-done | bytes 4194320 | tf_op jit(solution)/shard_map/reduce_scatter | solution.py:223
  838.9 5.2 all-gather.11
  844.3 39.8 %all-gather.25.cloned.1.call-done = bf16[1024,3072]{1,0:T(8,128)(2,1)} async-done(((bf16[256,3072]{1,0:T(8,128)(2,1)}), bf16[1024,3072]{1,0:T(8,128)(2,1)}) %all-gather.25.cloned.1.call-update) | async-done | bytes 6291472 | tf_op jit(solution)/shard_map/all_gather | solution.py:138
  884.1 6.4 fusion.60
  891.3 1.6 convert_reduce_fusion.3
  892.9 11.6 all-reduce.13
  905.1 3.5 copy.49
  908.6 39.9 %all-reduce.11 = (f32[256]{0:T(256)}, f32[256]{0:T(256)}, f32[256]{0:T(256)}, f32[256]{0:T(256)}, f32[256]{0:T(256)}, /*index=5*/f32[256]{0:T(256)}, f32[256]{0:T(256)}, f32[1024]{0:T(1024)}, f32[256]{0:T(256)}) all-reduce(f32[256]{0:T(256)S(1)} %dynamic-slice.7, ...), channel_id=1, replica_groups=mesh['seq'=2,'shard'=4,'rep'=4] {'seq','rep'}, use_global_device_ids=true, to_apply=%region_17.18 | all-reduce | flops 3072 | bytes 24576 | tf_op jit(solution)/shard_map/psum | solution.py:226
  948.5 7.7 fusion.28
  956.2 328.6 %all-reduce.18.cloned.1.call-done = (f32[256,3072]{1,0:T(8,128)}, f32[256,1024]{1,0:T(8,128)}, f32[256,4096]{1,0:T(8,128)}, f32[1024,1024]{1,0:T(8,128)}) async-done(((f32[256,3072]{1,0:T(8,128)}, f32[256,1024]{1,0:T(8,128)}, f32[256,4096]{1,0:T(8,128)}, f32[1024,1024]{1,0:T(8,128)}), (f32[256,3072]{1,0:T(8,128)}, f32[256,1024]{1,0:T(8,128)}, f32[256,4096]{1,0:T(8,128)}, ...) | async-done | bytes 12582928 | tf_op jit(solution)/shard_map/psum | solution.py:226
  1284.8 4.0 copy.67
  1289.8 2.1 copy.69
  1291.9 1.6 copy-done.11
  1293.5 2.0 copy.70
  (145 shorter events, 20.7 us)
Async XLA Ops:
  7.2 67.0 %copy-start.6 = (bf16[256,3072]{1,0:T(8,128)(2,1)S(1)}, bf16[256,3072]{1,0:T(8,128)(2,1)}, u32[]{:S(2)}) copy-start(bf16[256,3072]{1,0:T(8,128)(2,1)} %param.18) | copy-start | bytes 4718596
  7.2 114.4 %all-gather.29.cloned.1.call-start = ((), (), s32[]{:S(2)}) async-start(), calls=%async_computation.13 | async-start | bytes 1818624 | tf_op jit(solution)/shard_map/all_gather | solution.py:102
  7.2 35.1 %collective-permute-start = (bf16[256,3072]{1,0:T(8,128)(2,1)}, bf16[256,3072]{1,0:T(8,128)(2,1)}, u32[]{:S(2)}, u32[]{:S(2)}) collective-permute-start(bf16[256,3072]{1,0:T(8,128)(2,1)} %param.18), channel_id=1, source_target_pairs={{0,4},{4,8},{8,12},{12,0},{1,5},{5,9},{9,13},{13,1},{2,6},{6,10},{... | collective-permute-start | bytes 4718600 | tf_op jit(solution)/shard_map/ppermute | solution.py:18
  7.8 68.3 %collective-permute-start.1 = (bf16[256,3072]{1,0:T(8,128)(2,1)}, bf16[256,3072]{1,0:T(8,128)(2,1)}, u32[]{:S(2)}, u32[]{:S(2)}) collective-permute-start(bf16[256,3072]{1,0:T(8,128)(2,1)} %param.18), channel_id=1, source_target_pairs={{0,12},{4,0},{8,4},{12,8},{1,13},{5,1},{9,5},{13,9},{2,14},{6,2},{... | collective-permute-start | bytes 4718600 | tf_op jit(solution)/shard_map/ppermute | solution.py:21
  42.4 35.3 %collective-permute-start.2 = (bf16[256,3072]{1,0:T(8,128)(2,1)}, bf16[256,3072]{1,0:T(8,128)(2,1)}, u32[]{:S(2)}, u32[]{:S(2)}) collective-permute-start(bf16[256,3072]{1,0:T(8,128)(2,1)} %collective-permute-done), channel_id=1, source_target_pairs={{0,4},{4,8},{8,12},{12,0},{1,5},{5,9},{9,13},{13,1},{2,6},{6,10},{... | collective-permute-start | bytes 4718600 | tf_op jit(solution)/shard_map/ppermute | solution.py:18
  73.4 1.0 copy-start.21
  74.4 4.9 copy-start.2
  79.3 5.1 copy-start.24
  79.3 10.4 copy-start.25
  81.6 1.8 copy-start.16
  84.4 49.4 %all-gather.27.cloned.1.call-start = ((), (), s32[]{:S(2)}) async-start(), calls=%async_computation.12 | async-start | bytes 1818624 | tf_op jit(solution)/shard_map/all_gather | solution.py:105
  94.8 5.5 copy-start.26
  94.8 10.6 copy-start.27
  94.8 15.6 %copy-start.28 = (bf16[256]{0:T(256)(128)(2,1)S(1)}, bf16[256]{0:T(256)(128)(2,1)}, u32[]{:S(2)}) copy-start(bf16[256]{0:T(256)(128)(2,1)} %param.26) | copy-start | bytes 1540
  94.8 20.7 %copy-start.23 = (bf16[1024]{0:T(1024)(128)(2,1)S(1)}, bf16[1024]{0:T(1024)(128)(2,1)}, u32[]{:S(2)}) copy-start(bf16[1024]{0:T(1024)(128)(2,1)} %param.28) | copy-start | bytes 6148
  97.6 60.3 %all-gather.19.cloned.1.call-start = ((), (), s32[]{:S(2)}) async-start(), calls=%async_computation.4 | async-start | bytes 2621440 | tf_op jit(solution)/shard_map/all_gather | solution.py:77
  98.4 119.3 %all-gather.21.cloned.1.call-start = ((), (), s32[]{:S(2)}) async-start(), calls=%async_computation.5 | async-start | bytes 10485760 | tf_op jit(solution)/shard_map/all_gather | solution.py:78
  98.9 178.4 %all-gather.23.cloned.1.call-start = ((), (), s32[]{:S(2)}) async-start(), calls=%async_computation.6 | async-start | bytes 10485760 | tf_op jit(solution)/shard_map/all_gather | solution.py:79
  99.5 408.4 %reduce-scatter.9.cloned.1.call-start = ((), (), s32[]{:S(2)}) async-start(), calls=%async_computation.9 | async-start | bytes 5242880 | tf_op jit(solution)/shard_map/reduce_scatter | solution.py:215
  146.8 4.5 copy-start
  146.8 4.5 copy-start.10
  288.0 6.4 copy-start.17
  288.0 8.0 copy-start.7
  294.9 1.1 copy-start.4
  296.3 0.8 copy-start.18
  300.3 0.7 copy-start.31
  300.3 1.9 copy-start.19
  300.4 280.7 %reduce-scatter.7.cloned.1.call-start = ((), (), s32[]{:S(2)}) async-start(), calls=%async_computation.8 | async-start | bytes 15728640 | tf_op jit(solution)/shard_map/reduce_scatter | solution.py:212
  307.0 12.6 slice-start
  307.0 12.6 slice-start.1
  307.0 14.1 %slice-start.2 = ((s8[12124160]{0:T(1024)(128)(4,1)}), s8[3735552]{0:T(1024)(128)(4,1)S(1)}, s32[]{:S(2)}) async-start(s8[12124160]{0:T(1024)(128)(4,1)} %bitcast.131), calls=%async_computation.17 | async-start | bytes 7471104
  327.7 2.6 copy-start.1
  337.4 129.2 %copy-start.3 = (bf16[580,16,64]{0,2,1:T(8,128)(2,1)S(1)}, bf16[580,16,64]{0,2,1:T(8,128)(2,1)}, u32[]{:S(2)}) copy-start(bf16[580,16,64]{0,2,1:T(8,128)(2,1)} %reshape.246) | copy-start | bytes 3563524
  464.7 6.9 copy-start.14
  466.6 5.0 copy-start.15
  471.6 0.9 copy-start.13
  481.9 226.8 %reduce-scatter.11.cloned.1.call-start = ((), (), s32[]{:S(2)}) async-start(), calls=%async_computation.10 | async-start | bytes 20971520 | tf_op jit(solution)/shard_map/reduce_scatter | solution.py:221
  495.7 1.2 copy-start.8
  495.7 340.6 %reduce-scatter.13.cloned.1.call-start = ((), (), s32[]{:S(2)}) async-start(), calls=%async_computation.11 | async-start | bytes 20971520 | tf_op jit(solution)/shard_map/reduce_scatter | solution.py:223
  507.3 376.8 %all-gather.25.cloned.1.call-start = ((), (), s32[]{:S(2)}) async-start(), calls=%async_computation.7 | async-start | bytes 7864320 | tf_op jit(solution)/shard_map/all_gather | solution.py:138
  507.9 776.9 %all-reduce.18.cloned.1.call-start = ((), (), s32[]{:S(2)}) async-start(), calls=%async_computation.14 | async-start | bytes 25165824 | tf_op jit(solution)/shard_map/psum | solution.py:226
  836.4 0.7 copy-start.30
  836.4 2.5 copy-start.29
  844.3 46.3 %copy-start.22 = (f32[290]{0:T(512)S(1)}, f32[290]{0:T(512)}, u32[]{:S(2)}) copy-start(f32[290]{0:T(512)} %copy-done.21) | copy-start | bytes 3484
  844.3 47.0 %copy-start.5 = (f32[290,1024]{1,0:T(8,128)S(1)}, f32[290,1024]{1,0:T(8,128)}, u32[]{:S(2)}) copy-start(f32[290,1024]{1,0:T(8,128)} %copy-done.4) | copy-start | bytes 3563524
  884.1 7.1 copy-start.9
  1284.8 4.0 copy-start.20
  1284.8 5.0 copy-start.12
  1289.8 3.7 copy-start.11
Sparse Core Ops, SparseCore 0:
  84.5 23.9 all-gather.28
  110.6 23.1 all-gather.26
  135.4 22.5 all-gather.18
  159.4 58.2 all-gather.20
  219.1 58.2 all-gather.22
  300.5 44.5 reduce-scatter.8
  482.0 98.9 reduce-scatter.6
  583.6 125.0 reduce-scatter.10
  711.3 125.0 reduce-scatter.12
  837.8 46.3 all-gather.24
  888.9 395.8 all-reduce.17
